TPU v7x, 512 devices: a whole 4x4x16 slice. The times are simulated.
512 devices in a mesh: loop: 64 (over z_lo, x, core), rep: 8 (over y, z_hi).
Axes of the slice: x: 4, y: 4, z: 16 (z_hi: 2, z_lo: 8; z = z_hi * 8 + z_lo), core: 2. Of those that a mesh axis runs over, the one named last changes fastest.
Arguments:
- features: bfloat16 [65536, 256], P(('loop', 'rep')), may hold values from -6 to 6
- weight: bfloat16 [256, 256], replicated, may hold values from -0.375 to 0.375
- tile_values: bfloat16 [49152, 128, 128], P(('loop', 'rep')), may hold values from -0.375 to 0.375
- tile_coords: int32 [49152, 2], P(('loop', 'rep')), may hold values from 0 to 7
- tile_counts: int32 [512, 8], P(('loop', 'rep')), may hold values from 1 to 12, as said below
Outputs:
- activated: bfloat16 [65536, 256], P(('loop', 'rep'))
Inputs may be any that keep to these rules, and one draw needn't show every extreme that they name: `tile_counts`: some list uses all 12 slots at some step; loads differ strongly between lists. `tile_coords`: row block within the group's rows and column block within the slab of that step.
All inputs are finite; a program needn't handle non-finite values.
Results may differ from a plain program's by a relative error of at most 0.0049.
Values may be sent and summed in bfloat16 or wider, within the bound.
A program may use at most 64 MiB of HBM per device.

v0:
```python
import jax
import jax.numpy as jnp
from jax import lax
from jax.sharding import PartitionSpec as P


def from_behind(x, axis, by):
    count = lax.axis_size(axis)
    return lax.ppermute(x, axis, [(i, (i + by) % count) for i in range(count)])


def local(features, weight, tile_values, tile_coords, tile_counts):
    rep_size = lax.axis_size("rep")
    loop_size = lax.axis_size("loop")
    step_count = loop_size // rep_size
    tile_size = tile_values.shape[1]
    feat_width = features.shape[1]
    slot_count = tile_values.shape[0] // step_count
    current_slab = lax.all_gather(features, "rep", axis=0, tiled=True)
    block_count = current_slab.shape[0] // tile_size
    values = tile_values.reshape(step_count, slot_count, tile_size, tile_size)
    coords = tile_coords.reshape(step_count, slot_count, 2)
    counts = tile_counts.reshape(step_count)
    rep_rank = lax.axis_index("rep")
    for bit_index in range(rep_size.bit_length() - 1):
        shifted = from_behind(current_slab, "loop", step_count * (1 << bit_index))
        current_slab = jnp.where(rep_rank >> bit_index & 1 == 1, shifted, current_slab)
    running = jnp.zeros((block_count, tile_size, feat_width), jnp.float32)
    for step_index in range(step_count):
        slab_blocks = current_slab.reshape(block_count, tile_size, feat_width)
        pieces = jnp.take(slab_blocks, coords[step_index, :, 1], axis=0)
        products = jnp.einsum(
            "ktc,kcf->ktf", values[step_index], pieces, preferred_element_type=jnp.float32
        )
        live_slot = (jnp.arange(slot_count) < counts[step_index]).astype(jnp.float32)
        running = running.at[coords[step_index, :, 0]].add(products * live_slot[:, None, None])
        if step_index + 1 < step_count:
            current_slab = from_behind(current_slab, "loop", 1)
    summed = lax.psum_scatter(
        running.reshape(block_count * tile_size, feat_width), "rep", scatter_dimension=0, tiled=True
    )
    aggregated = summed.astype(jnp.bfloat16)
    product = jnp.dot(aggregated, weight, preferred_element_type=jnp.float32)
    return jnp.maximum(product, 0.0).astype(jnp.bfloat16)


def solution(mesh):
    placed = (
        P(("loop", "rep"), None),
        P(),
        P(("loop", "rep"), None, None),
        P(("loop", "rep"), None),
        P(("loop", "rep"), None),
    )
    return jax.shard_map(
        local, mesh=mesh, in_specs=placed, out_specs=P(("loop", "rep"), None), check_vma=False
    )
```

profile of v0, /device:TPU:7, one launch (start us, length us, event | category | flops | bytes accessed | tf_op | source)
XLA Modules:
  0.0 453.7 jit_solution(15041202940088888313)
XLA Ops:
  6.5 83.0 %all_gather.3 = bf16[1024,256]{1,0:T(8,128)(2,1)S(1)} all-gather(bf16[128,256]{1,0:T(8,128)(2,1)} %param.7), channel_id=1, replica_groups=mesh['loop'=64,'rep'=8] {'rep'}, dimensions={0}, use_global_device_ids=true | all-gather | bytes 589824 | tf_op jit(solution)/shard_map/all_gather | solution.py:19
  89.5 1.9 collective-permute-start
  91.5 14.7 %collective-permute-done = bf16[1024,256]{1,0:T(8,128)(2,1)S(1)} collective-permute-done((bf16[1024,256]{1,0:T(8,128)(2,1)S(1)}, bf16[1024,256]{1,0:T(8,128)(2,1)S(1)}, u32[]{:S(2)}, u32[]{:S(2)}) %collective-permute-start) | collective-permute-done | bytes 524320 | tf_op jit(solution)/shard_map/ppermute | solution.py:9
  106.2 1.9 collective-permute-start.1
  108.1 17.6 %collective-permute-done.1 = bf16[1024,256]{1,0:T(8,128)(2,1)S(1)} collective-permute-done((bf16[1024,256]{1,0:T(8,128)(2,1)S(1)}, bf16[1024,256]{1,0:T(8,128)(2,1)S(1)}, u32[]{:S(2)}, u32[]{:S(2)}) %collective-permute-start.1) | collective-permute-done | bytes 524320 | tf_op jit(solution)/shard_map/ppermute | solution.py:9
  125.8 1.9 collective-permute-start.2
  127.8 0.7 fusion.50
  128.5 0.6 compare_convert_fusion.7
  129.1 1.2 compare_convert_fusion.6
  130.3 42.9 %collective-permute-done.2 = bf16[1024,256]{1,0:T(8,128)(2,1)S(1)} collective-permute-done((bf16[1024,256]{1,0:T(8,128)(2,1)S(1)}, bf16[1024,256]{1,0:T(8,128)(2,1)S(1)}, u32[]{:S(2)}, u32[]{:S(2)}) %collective-permute-start.2) | collective-permute-done | bytes 524320 | tf_op jit(solution)/shard_map/ppermute | solution.py:9
  173.3 1.9 collective-permute-start.3
  175.2 1.2 compare_convert_fusion.5
  176.4 1.1 compare_convert_fusion.4
  177.6 1.2 compare_convert_fusion.3
  178.8 0.6 compare_and_fusion
  179.4 2.0 collective-permute-done.3
  181.3 6.5 %collective-permute-start.4 = (bf16[1024,256]{1,0:T(8,128)(2,1)S(1)}, bf16[1024,256]{1,0:T(8,128)(2,1)S(1)}, u32[]{:S(2)}, u32[]{:S(2)}) collective-permute-start(bf16[1024,256]{1,0:T(8,128)(2,1)S(1)} %collective-permute-done.3), channel_id=1, source_target_pairs={{0,8},{8,16},{16,24},{24,32},{32,40},{40,48},{48,56},{56,64},{64,7... | collective-permute-start | bytes 1572872 | tf_op jit(solution)/shard_map/ppermute | solution.py:9
  187.8 1.2 compare_convert_fusion.2
  189.0 0.6 pad_clamp_fusion.6
  190.8 3.1 collective-permute-done.4
  193.9 13.2 %collective-permute-start.5 = (bf16[1024,256]{1,0:T(8,128)(2,1)S(1)}, bf16[1024,256]{1,0:T(8,128)(2,1)}, u32[]{:S(2)}, u32[]{:S(2)}) collective-permute-start(bf16[1024,256]{1,0:T(8,128)(2,1)S(1)} %collective-permute-done.4), channel_id=1, source_target_pairs={{0,8},{8,16},{16,24},{24,32},{32,40},{40,48},{48,56},{56,64},{64,7... | collective-permute-start | bytes 1572872 | tf_op jit(solution)/shard_map/ppermute | solution.py:9
  207.2 1.1 compare_convert_fusion.1
  208.3 5.0 %collective-permute-done.5 = bf16[1024,256]{1,0:T(8,128)(2,1)} collective-permute-done((bf16[1024,256]{1,0:T(8,128)(2,1)S(1)}, bf16[1024,256]{1,0:T(8,128)(2,1)}, u32[]{:S(2)}, u32[]{:S(2)}) %collective-permute-start.5) | collective-permute-done | bytes 524320 | tf_op jit(solution)/shard_map/ppermute | solution.py:9
  213.3 6.6 %collective-permute-start.6 = (bf16[1024,256]{1,0:T(8,128)(2,1)}, bf16[1024,256]{1,0:T(8,128)(2,1)}, u32[]{:S(2)}, u32[]{:S(2)}) collective-permute-start(bf16[1024,256]{1,0:T(8,128)(2,1)} %collective-permute-done.5), channel_id=1, source_target_pairs={{0,8},{8,16},{16,24},{24,32},{32,40},{40,48},{48,56},{56,64},{64,7... | collective-permute-start | bytes 1572872 | tf_op jit(solution)/shard_map/ppermute | solution.py:9
  219.9 1.1 compare_convert_fusion
  221.0 0.6 fusion.41
  221.6 0.6 gather_fusion
  222.2 2.6 multiply_bitcast_fusion.7
  224.9 1.9 copy.33
  226.8 1.8 scatter_fusion
  228.7 1.8 gather_fusion.1
  230.5 5.3 %collective-permute-start.7 = (bf16[1024,256]{1,0:T(8,128)(2,1)}, bf16[1024,256]{1,0:T(8,128)(2,1)}, u32[]{:S(2)}, u32[]{:S(2)}) collective-permute-start(bf16[1024,256]{1,0:T(8,128)(2,1)} %collective-permute-done.6), channel_id=1, source_target_pairs={{0,8},{8,16},{16,24},{24,32},{32,40},{40,48},{48,56},{56,64},{64,7... | collective-permute-start | bytes 1572872 | tf_op jit(solution)/shard_map/ppermute | solution.py:9
  235.8 1.5 multiply_bitcast_fusion.6
  237.3 1.6 copy.37
  238.9 3.1 scatter_fusion.1
  242.0 0.7 gather_fusion.2
  242.8 1.5 multiply_bitcast_fusion.5
  244.3 1.6 copy.41
  245.9 3.1 scatter_fusion.2
  249.0 1.8 gather_fusion.3
  250.8 4.7 %collective-permute-start.8 = (bf16[1024,256]{1,0:T(8,128)(2,1)}, bf16[1024,256]{1,0:T(8,128)(2,1)}, u32[]{:S(2)}, u32[]{:S(2)}) collective-permute-start(bf16[1024,256]{1,0:T(8,128)(2,1)} %collective-permute-done.7), channel_id=1, source_target_pairs={{0,8},{8,16},{16,24},{24,32},{32,40},{40,48},{48,56},{56,64},{64,7... | collective-permute-start | bytes 1572872 | tf_op jit(solution)/shard_map/ppermute | solution.py:9
  255.5 1.5 multiply_bitcast_fusion.4
  257.0 1.6 copy.45
  258.6 3.1 scatter_fusion.3
  261.7 1.6 gather_fusion.4
  263.4 1.5 multiply_bitcast_fusion.3
  264.9 1.6 copy.49
  266.5 3.1 scatter_fusion.4
  269.6 1.6 gather_fusion.5
  271.3 1.9 collective-permute-start.9
  273.2 1.5 multiply_bitcast_fusion.2
  274.7 1.6 copy.53
  276.4 3.1 scatter_fusion.5
  279.5 1.6 gather_fusion.6
  281.2 1.5 multiply_bitcast_fusion.1
  282.7 1.6 copy.57
  284.3 3.1 scatter_fusion.6
  287.5 1.6 gather_fusion.7
  289.1 2.6 multiply_bitcast_fusion
  291.8 1.9 copy.61
  293.7 1.8 scatter_fusion.7
  295.5 1.0 copy-done.1
  296.5 148.7 %reduce-scatter.2.cloned.1.call-done = f32[128,256]{1,0:T(8,128)} async-done(((f32[1024,256]{1,0:T(8,128)}), f32[128,256]{1,0:T(8,128)}) %reduce-scatter.2.cloned.1.call-update) | async-done | bytes 131088 | tf_op jit(solution)/shard_map/reduce_scatter | solution.py:39
  445.2 1.7 fusion
  (55 shorter events, 1.7 us)
Async XLA Ops:
  6.5 438.6 %copy-start = (bf16[256,256]{1,0:T(8,128)(2,1)S(1)}, bf16[256,256]{1,0:T(8,128)(2,1)}, u32[]{:S(2)}) copy-start(bf16[256,256]{1,0:T(8,128)(2,1)} %param.8) | copy-start | bytes 393220
  6.5 438.6 %reduce-scatter.2.cloned.1.call-start = ((), (), s32[]{:S(2)}) async-start(), calls=%async_computation.1 | async-start | bytes 1179648 | tf_op jit(solution)/shard_map/reduce_scatter | solution.py:39
  89.5 16.6 %collective-permute-start = (bf16[1024,256]{1,0:T(8,128)(2,1)S(1)}, bf16[1024,256]{1,0:T(8,128)(2,1)S(1)}, u32[]{:S(2)}, u32[]{:S(2)}) collective-permute-start(bf16[1024,256]{1,0:T(8,128)(2,1)S(1)} %all_gather.3), channel_id=1, source_target_pairs={{0,64},{8,72},{16,80},{24,88},{32,96},{40,104},{48,112},{56,120},{... | collective-permute-start | bytes 1572872 | tf_op jit(solution)/shard_map/ppermute | solution.py:9
  91.4 36.3 %copy-start.16 = (s32[96,2]{0,1:T(2,128)S(1)}, s32[96,2]{0,1:T(2,128)}, u32[]{:S(2)}) copy-start(s32[96,2]{0,1:T(2,128)} %param.10) | copy-start | bytes 2308
  91.5 36.3 %copy-start.5 = (s32[1,8]{1,0:T(1,128)S(1)}, s32[1,8]{1,0:T(1,128)}, u32[]{:S(2)}) copy-start(s32[1,8]{1,0:T(1,128)} %param.11) | copy-start | bytes 100
  106.2 19.5 %collective-permute-start.1 = (bf16[1024,256]{1,0:T(8,128)(2,1)S(1)}, bf16[1024,256]{1,0:T(8,128)(2,1)S(1)}, u32[]{:S(2)}, u32[]{:S(2)}) collective-permute-start(bf16[1024,256]{1,0:T(8,128)(2,1)S(1)} %broadcast_select_fusion), channel_id=1, source_target_pairs={{0,128},{8,136},{16,144},{24,152},{32,160},{40,168},{48,176},{56,1... | collective-permute-start | bytes 1572872 | tf_op jit(solution)/shard_map/ppermute | solution.py:9
  125.8 47.5 %collective-permute-start.2 = (bf16[1024,256]{1,0:T(8,128)(2,1)S(1)}, bf16[1024,256]{1,0:T(8,128)(2,1)S(1)}, u32[]{:S(2)}, u32[]{:S(2)}) collective-permute-start(bf16[1024,256]{1,0:T(8,128)(2,1)S(1)} %broadcast_select_fusion.1), channel_id=1, source_target_pairs={{0,256},{8,264},{16,272},{24,280},{32,288},{40,296},{48,304},{56,3... | collective-permute-start | bytes 1572872 | tf_op jit(solution)/shard_map/ppermute | solution.py:9
  173.3 8.0 %collective-permute-start.3 = (bf16[1024,256]{1,0:T(8,128)(2,1)S(1)}, bf16[1024,256]{1,0:T(8,128)(2,1)S(1)}, u32[]{:S(2)}, u32[]{:S(2)}) collective-permute-start(bf16[1024,256]{1,0:T(8,128)(2,1)S(1)} %broadcast_select_fusion.2), channel_id=1, source_target_pairs={{0,8},{8,16},{16,24},{24,32},{32,40},{40,48},{48,56},{56,64},{64,7... | collective-permute-start | bytes 1572872 | tf_op jit(solution)/shard_map/ppermute | solution.py:9
  181.3 43.5 %copy-start.2 = (bf16[1024,256]{1,0:T(8,128)(2,1)}, bf16[1024,256]{1,0:T(8,128)(2,1)S(1)}, u32[]{:S(2)}) copy-start(bf16[1024,256]{1,0:T(8,128)(2,1)S(1)} %collective-permute-done.3) | copy-start | bytes 1572868
  181.3 12.6 %collective-permute-start.4 = (bf16[1024,256]{1,0:T(8,128)(2,1)S(1)}, bf16[1024,256]{1,0:T(8,128)(2,1)S(1)}, u32[]{:S(2)}, u32[]{:S(2)}) collective-permute-start(bf16[1024,256]{1,0:T(8,128)(2,1)S(1)} %collective-permute-done.3), channel_id=1, source_target_pairs={{0,8},{8,16},{16,24},{24,32},{32,40},{40,48},{48,56},{56,64},{64,7... | collective-permute-start | bytes 1572872 | tf_op jit(solution)/shard_map/ppermute | solution.py:9
  193.9 27.7 %copy-start.3 = (bf16[1024,256]{1,0:T(8,128)(2,1)}, bf16[1024,256]{1,0:T(8,128)(2,1)S(1)}, u32[]{:S(2)}) copy-start(bf16[1024,256]{1,0:T(8,128)(2,1)S(1)} %collective-permute-done.4) | copy-start | bytes 1572868
  193.9 19.4 %collective-permute-start.5 = (bf16[1024,256]{1,0:T(8,128)(2,1)S(1)}, bf16[1024,256]{1,0:T(8,128)(2,1)}, u32[]{:S(2)}, u32[]{:S(2)}) collective-permute-start(bf16[1024,256]{1,0:T(8,128)(2,1)S(1)} %collective-permute-done.4), channel_id=1, source_target_pairs={{0,8},{8,16},{16,24},{24,32},{32,40},{40,48},{48,56},{56,64},{64,7... | collective-permute-start | bytes 1572872 | tf_op jit(solution)/shard_map/ppermute | solution.py:9
  213.3 17.2 %collective-permute-start.6 = (bf16[1024,256]{1,0:T(8,128)(2,1)}, bf16[1024,256]{1,0:T(8,128)(2,1)}, u32[]{:S(2)}, u32[]{:S(2)}) collective-permute-start(bf16[1024,256]{1,0:T(8,128)(2,1)} %collective-permute-done.5), channel_id=1, source_target_pairs={{0,8},{8,16},{16,24},{24,32},{32,40},{40,48},{48,56},{56,64},{64,7... | collective-permute-start | bytes 1572872 | tf_op jit(solution)/shard_map/ppermute | solution.py:9
  230.5 20.3 %collective-permute-start.7 = (bf16[1024,256]{1,0:T(8,128)(2,1)}, bf16[1024,256]{1,0:T(8,128)(2,1)}, u32[]{:S(2)}, u32[]{:S(2)}) collective-permute-start(bf16[1024,256]{1,0:T(8,128)(2,1)} %collective-permute-done.6), channel_id=1, source_target_pairs={{0,8},{8,16},{16,24},{24,32},{32,40},{40,48},{48,56},{56,64},{64,7... | collective-permute-start | bytes 1572872 | tf_op jit(solution)/shard_map/ppermute | solution.py:9
  237.3 1.6 copy-start.15
  238.9 3.1 copy-start.4
  244.3 1.6 copy-start.14
  250.8 20.5 %collective-permute-start.8 = (bf16[1024,256]{1,0:T(8,128)(2,1)}, bf16[1024,256]{1,0:T(8,128)(2,1)}, u32[]{:S(2)}, u32[]{:S(2)}) collective-permute-start(bf16[1024,256]{1,0:T(8,128)(2,1)} %collective-permute-done.7), channel_id=1, source_target_pairs={{0,8},{8,16},{16,24},{24,32},{32,40},{40,48},{48,56},{56,64},{64,7... | collective-permute-start | bytes 1572872 | tf_op jit(solution)/shard_map/ppermute | solution.py:9
  257.0 1.6 copy-start.13
  264.9 1.6 copy-start.12
  269.6 3.6 copy-start.8
  271.3 16.2 %collective-permute-start.9 = (bf16[1024,256]{1,0:T(8,128)(2,1)}, bf16[1024,256]{1,0:T(8,128)(2,1)}, u32[]{:S(2)}, u32[]{:S(2)}) collective-permute-start(bf16[1024,256]{1,0:T(8,128)(2,1)} %collective-permute-done.8), channel_id=1, source_target_pairs={{0,8},{8,16},{16,24},{24,32},{32,40},{40,48},{48,56},{56,64},{64,7... | collective-permute-start | bytes 1572872 | tf_op jit(solution)/shard_map/ppermute | solution.py:9
  274.7 1.6 copy-start.11
  279.5 1.7 copy-start.7
  279.5 1.7 copy-start.17
  282.7 1.6 copy-start.10
  287.4 1.7 copy-start.6
  287.4 1.7 copy-start.18
  291.8 1.9 copy-start.9
  295.5 1.0 copy-start.1
Sparse Core Ops, SparseCore 0:
  296.6 148.4 reduce-scatter.1
where the time goes:
time: 457 us; the launch traced here: 454 us
  waiting for transfers between devices  234 us (51%)
  blocking collectives  83 us (18%)
  starting transfers between devices  45.9 us (10%)
  other arithmetic  34.3 us (8%)
  local copies, waits for them, and re-layouts  26.7 us (6%)
  matrix products  15.9 us (3%)
  between operations  13.9 us (3%)
    reduce_scatter x1, waiting for transfers between devices, local(): lax.psum_scatter(running.reshape(block_count * tile_size, feat_width), 'r...  149 us
    ppermute x10, waiting for transfers between devices, from_behind(): return lax.ppermute(x, axis, [(i, (i + by) % count) for i in range(count)])  85.3 us
    all_gather x1, blocking collectives, local(): current_slab = lax.all_gather(features, 'rep', axis=0, tiled=True)  83 us
    ppermute x10, starting transfers between devices, from_behind(): return lax.ppermute(x, axis, [(i, (i + by) % count) for i in range(count)])  45.9 us
    scatter-add x8, other arithmetic, local(): running.at[coords[step_index, :, 0]]  22.4 us
    dot_general x8, matrix products, local(): jnp.einsum('ktc,kcf->ktf', values[step_index], pieces, preferred_element_...  14.2 us
    mul x8, local copies, waits for them, and re-layouts, local(): products * live_slot[:, None, None]  13.5 us
    gather x8, local copies, waits for them, and re-layouts, local(): pieces = jnp.take(slab_blocks, coords[step_index, :, 1], axis=0)  11.4 us
  transfers between devices with their start and end apart: 11, of which 7 were waited for; matrix products, arithmetic and copies ran while one was open for 15% of the time, Pallas kernels for 0%

commit v1 on v0

v1 whole, which is shorter than its diff:
```python
import functools

import jax
import jax.numpy as jnp
from jax import lax
from jax.experimental import pallas as pl
from jax.experimental.pallas import tpu as pltpu
from jax.sharding import PartitionSpec as P

MESH = pl.DeviceIdType.MESH
NX, NY, NZ, NC, NZH, NZL = 4, 4, 16, 2, 2, 8


def place():
    l = lax.axis_index("loop")
    r = lax.axis_index("rep")
    zl, x, core = l // (NX * NC), (l // NC) % NX, l % NC
    y, zh = r // NZH, r % NZH
    return x, core, y, zh * NZL + zl


def device(x, core, y, z):
    return ((z % NZL) * (NX * NC) + x * NC + core, y * NZH + z // NZL)


def greet(targets):
    barrier = pltpu.get_barrier_semaphore()
    for target in targets:
        pl.semaphore_signal(barrier, inc=1, device_id=target, device_id_type=MESH)
    pl.semaphore_wait(barrier, len(targets))


def gather_kernel(
    own, out, feat, up, down,
    up_send, up_recv, down_send, down_recv,
    y_send, y_recv, y_local, x_send, x_recv, f_send, f_recv, s_send, s_recv, o_sem,
):
    x, core, y, z = place()
    zl, zh = z % NZL, z // NZL
    xp, xm = (x + 1) % NX, (x + NX - 1) % NX
    xo = (x + 2) % NX
    zp, zm = (z + 1) % NZ, (z + NZ - 1) % NZ
    right, left = device(xp, core, y, z), device(xm, core, y, z)
    above, below = device(x, core, y, zp), device(x, core, y, zm)
    sibling = device(x, 1 - core, y, z)
    others = [(y + d) % NY for d in range(1, NY)]
    mine = x * NC + core

    def remote(src, dst, send, recv, target):
        return pltpu.make_async_remote_copy(
            src_ref=src, dst_ref=dst, send_sem=send, recv_sem=recv,
            device_id=target, device_id_type=MESH,
        )

    greet([right, left, above, below, sibling] + [device(x, core, v, z) for v in others])

    def goes(plane):
        offset = (zl + NZL - zh + NZL - plane % NZL) % NZL
        return offset // 2, offset % 2, plane // NZL

    def slab(kind):
        return (1 - kind) * mine + kind * (NX * NC)

    def hand_on(src, plane, index):
        reader, kind, half = goes(plane)
        dst = feat.at[slab(kind), half, y]

        @pl.when(reader == y)
        def _():
            pltpu.make_async_copy(src, dst, y_local.at[kind * 2 + half]).start()

        @pl.when(reader != y)
        def _():
            remote(
                src, dst, y_send.at[index], y_recv.at[kind * 2 + half, y],
                device(x, core, reader, z),
            ).start()

    def hand_on_done(src, plane, index):
        reader, kind, half = goes(plane)

        @pl.when(reader != y)
        def _():
            remote(
                src, feat.at[slab(kind), half, y], y_send.at[index],
                y_recv.at[kind * 2 + half, y], device(x, core, reader, z),
            ).wait_send()

    def x_copy(kind, half, direction):
        return remote(
            feat.at[slab(kind), half], feat.at[mine, half],
            x_send.at[direction, kind * 2 + half], x_recv.at[x, half],
            right if direction == 0 else left,
        )

    def share_copy(src, other, half):
        return remote(
            feat.at[src, half], feat.at[other * NC + core, half],
            s_send.at[other, half], s_recv.at[other, half], sibling,
        )

    def rightward(kind):
        return jnp.where(kind == 0, (x < NX - 1).astype(jnp.int32), (x == NX - 1).astype(jnp.int32)) == 1

    def leftward(kind):
        return jnp.where(kind == 0, (x == 0).astype(jnp.int32), (x > 0).astype(jnp.int32)) == 1

    def complete(src, plane):
        reader, kind, half = goes(plane)

        @pl.when(reader == y)
        def _():
            for v in others:
                remote(
                    src, feat.at[slab(kind), half, v], y_send.at[0],
                    y_recv.at[kind * 2 + half, v], sibling,
                ).wait_recv()
            pltpu.make_async_copy(
                src, feat.at[slab(kind), half, y], y_local.at[kind * 2 + half]
            ).wait()

            @pl.when(rightward(kind))
            def _():
                x_copy(kind, half, 0).start()

            @pl.when(leftward(kind))
            def _():
                x_copy(kind, half, 1).start()

            @pl.when(kind == core)
            def _():
                share_copy(slab(kind), x, half).start()

    def z_copy(src, step, upward):
        if upward:
            return remote(src, up.at[step], up_send.at[step], up_recv.at[step], above)
        return remote(src, down.at[step], down_send.at[step], down_recv.at[step], below)

    z_copy(own, 1, True).start()
    z_copy(own, 1, False).start()
    hand_on(own, z, 0)

    far = NZ // 2

    def step_body(t, carry):
        plane_up, plane_down = (z + NZ - t) % NZ, (z + t) % NZ
        z_copy(own, t, True).wait_recv()

        @pl.when(t < far)
        def _():
            z_copy(up.at[t], t + 1, True).start()
            z_copy(own, t, False).wait_recv()

            @pl.when(t < far - 1)
            def _():
                z_copy(down.at[t], t + 1, False).start()

        hand_on(up.at[t], plane_up, t)

        @pl.when(t < far)
        def _():
            hand_on(down.at[t], plane_down, far + t)

        @pl.when(t == 1)
        def _():
            complete(own, z)

        @pl.when(t > 1)
        def _():
            complete(own, (z + NZ - t + 1) % NZ)
            complete(own, (z + t - 1) % NZ)

        return carry

    lax.fori_loop(1, far + 1, step_body, 0)
    complete(own, (z + far) % NZ)

    plane_a = (zl + NZL - y * 2 - zh + NZL) % NZL
    gap = (z + NZ - plane_a) % NZ
    near = jnp.where(jnp.minimum(gap, NZ - gap) <= NZ // 4, 0, 1)

    def forward(source, half, piece, to_right):
        part = feat.at[source * NC + core, half, pl.ds(piece * 2, 2)]
        return remote(
            part, part, f_send.at[0 if to_right else 1, half, piece], f_recv.at[half, piece],
            right if to_right else left,
        )

    def arrived(source, half):
        remote(
            feat.at[mine, half], feat.at[source * NC + core, half],
            x_send.at[0, 0], x_recv.at[source, half], sibling,
        ).wait_recv()

    def out_copy(c, half):
        return pltpu.make_async_copy(feat.at[c, half], out.at[c, half], o_sem.at[c, half])

    moves = (
        (True, 0, x < NX - 1), (True, 1, x == 2), (False, 1, x > 0), (False, 0, x == 1),
    )

    for turn in range(2):
        half = jnp.where(near == turn, 0, 1)
        for to_right, source in ((True, xm), (False, xp)):
            arrived(source, half)
            for direction, piece, when in moves:
                if direction == to_right:
                    @pl.when(when)
                    def _(source=source, piece=piece, to_right=to_right):
                        forward(source, half, piece, to_right).start()
            share_copy(source * NC + core, source, half).start()
    for turn in range(2):
        half = jnp.where(near == turn, 0, 1)
        for piece in range(2):
            forward(xo, half, piece, True).wait_recv()
        share_copy(xo * NC + core, xo, half).start()
        for other in range(NX):
            out_copy(other * NC + core, half).start()
    for turn in range(2):
        half = jnp.where(near == turn, 0, 1)
        for other in (x, xm, xp, xo):
            c = other * NC + 1 - core
            remote(
                feat.at[c, half], feat.at[c, half], s_send.at[0, 0], s_recv.at[other, half], sibling
            ).wait_recv()
            out_copy(c, half).start()

    for half in range(2):
        for c in range(NX * NC):
            out_copy(c, half).wait()
        for other in range(NX):
            share_copy(other * NC + core, other, half).wait_send()
        for direction, piece, when in moves:
            @pl.when(when)
            def _(direction=direction, piece=piece, half=half):
                forward(xm if direction else xp, half, piece, direction).wait_send()
        for kind in range(2):
            @pl.when(rightward(kind))
            def _(kind=kind, half=half):
                x_copy(kind, half, 0).wait_send()

            @pl.when(leftward(kind))
            def _(kind=kind, half=half):
                x_copy(kind, half, 1).wait_send()
    hand_on_done(own, z, 0)

    def drain(t, carry):
        z_copy(own, t, True).wait_send()
        hand_on_done(up.at[t], (z + NZ - t) % NZ, t)

        @pl.when(t < far)
        def _():
            z_copy(own, t, False).wait_send()
            hand_on_done(down.at[t], (z + t) % NZ, far + t)

        return carry

    lax.fori_loop(1, far + 1, drain, 0)


def gather(features):
    rows, width = features.shape
    dma = pltpu.SemaphoreType.DMA
    kind = features.dtype
    return pl.pallas_call(
        gather_kernel,
        out_shape=jax.ShapeDtypeStruct((NX * NC, 2, NY, rows, width), kind),
        in_specs=[pl.BlockSpec(memory_space=pltpu.VMEM)],
        out_specs=pl.BlockSpec(memory_space=pl.ANY),
        scratch_shapes=[
            pltpu.VMEM((NX * NC + 1, 2, NY, rows, width), kind),
            pltpu.VMEM((NZ // 2 + 1, rows, width), kind),
            pltpu.VMEM((NZ // 2, rows, width), kind),
            dma((NZ // 2 + 1,)), dma((NZ // 2 + 1,)), dma((NZ // 2,)), dma((NZ // 2,)),
            dma((NZ,)), dma((4, NY)), dma((4,)),
            dma((2, 4)), dma((NX, 2)),
            dma((2, 2, 2)), dma((2, 2)),
            dma((NX, 2)), dma((NX, 2)),
            dma((NX * NC, 2)),
        ],
        compiler_params=pltpu.CompilerParams(collective_id=0, has_side_effects=True),
        name="gather",
    )(features)


def product_kernel(counts, coords, first, tiles, slab, out, acc, *, slots, blocks, steps):
    step = pl.program_id(0)

    @pl.when(step == 0)
    def _():
        acc[...] = jnp.zeros_like(acc)

    count = counts[step]
    for q in range(slots):
        at = (step * slots + q) * 2
        row = jnp.where(q < count, coords[at], blocks)
        b = coords[at + 1]
        spot = (b % NZH) * NY + b // NZH
        acc[row] += jnp.dot(tiles[q], slab[0, spot], preferred_element_type=jnp.float32)

    @pl.when(step == steps - 1)
    def _():
        out[...] = acc[:blocks].astype(out.dtype)


def products(tile_values, tile_coords, tile_counts, slabs):
    steps = tile_counts.shape[1]
    slots = tile_values.shape[0] // steps
    tile = tile_values.shape[1]
    width = slabs.shape[-1]
    blocks = slabs.shape[1] * slabs.shape[2]
    slabs = slabs.reshape(slabs.shape[0], blocks, tile, width)
    first = (lax.axis_index("loop") % (NX * NC)).reshape(1)
    grid = pltpu.PrefetchScalarGridSpec(
        num_scalar_prefetch=3,
        grid=(steps,),
        in_specs=[
            pl.BlockSpec((slots, tile, tile), lambda s, n, c, f: (s, 0, 0)),
            pl.BlockSpec(
                (1, blocks, tile, width), lambda s, n, c, f: ((f[0] + steps - s) % steps, 0, 0, 0)
            ),
        ],
        out_specs=pl.BlockSpec((blocks, tile, width), lambda s, n, c, f: (0, 0, 0)),
        scratch_shapes=[pltpu.VMEM((blocks + 1, tile, width), jnp.float32)],
    )
    return pl.pallas_call(
        functools.partial(product_kernel, slots=slots, blocks=blocks, steps=steps),
        grid_spec=grid,
        out_shape=jax.ShapeDtypeStruct((blocks, tile, width), slabs.dtype),
        name="products",
    )(tile_counts.reshape(-1), tile_coords.reshape(-1), first, tile_values, slabs)


def combine_kernel(part, weight, out, got, give, far, y_send, y_recv, z_send, z_recv):
    x, core, y, z = place()
    zh = z // NZL
    partner = device(x, core, y, (z + NZL) % NZ)
    others = [(y + d) % NY for d in range(1, NY)]
    greet([device(x, core, v, z) for v in others] + [partner])

    def y_copy(i, src):
        return pltpu.make_async_remote_copy(
            src_ref=part.at[others[i]], dst_ref=got.at[src], send_sem=y_send.at[i],
            recv_sem=y_recv.at[src], device_id=device(x, core, others[i], z), device_id_type=MESH,
        )

    for i in range(NY - 1):
        y_copy(i, y).start()
    for i in range(NY - 1):
        y_copy(i, others[i]).wait_recv()

    def total(half):
        held = part[y, half].astype(jnp.float32)
        for v in others:
            held += got[v, half].astype(jnp.float32)
        return held

    give[...] = total(1 - zh).astype(give.dtype)
    across = pltpu.make_async_remote_copy(
        src_ref=give, dst_ref=far, send_sem=z_send, recv_sem=z_recv,
        device_id=partner, device_id_type=MESH,
    )
    across.start()
    held = total(zh)
    across.wait()
    aggregated = (held + far[...].astype(jnp.float32)).astype(weight.dtype)
    product = jnp.dot(aggregated, weight[...], preferred_element_type=jnp.float32)
    out[...] = jnp.maximum(product, 0.0).astype(out.dtype)
    for i in range(NY - 1):
        y_copy(i, y).wait_send()


def combine(part, weight):
    blocks, rows, width = part.shape
    part = part.reshape(NY, NZH, rows, width)
    dma = pltpu.SemaphoreType.DMA
    return pl.pallas_call(
        combine_kernel,
        out_shape=jax.ShapeDtypeStruct((rows, weight.shape[1]), part.dtype),
        in_specs=[pl.BlockSpec(memory_space=pltpu.VMEM)] * 2,
        out_specs=pl.BlockSpec(memory_space=pltpu.VMEM),
        scratch_shapes=[
            pltpu.VMEM((NY, NZH, rows, width), part.dtype),
            pltpu.VMEM((rows, width), part.dtype),
            pltpu.VMEM((rows, width), part.dtype),
            dma((NY - 1,)), dma((NY,)), dma, dma,
        ],
        compiler_params=pltpu.CompilerParams(collective_id=1, has_side_effects=True),
        name="combine",
    )(part, weight)


def local(features, weight, tile_values, tile_coords, tile_counts):
    slabs = gather(features)
    part = products(tile_values, tile_coords, tile_counts, slabs)
    return combine(part, weight)


def solution(mesh):
    placed = (
        P(("loop", "rep"), None),
        P(),
        P(("loop", "rep"), None, None),
        P(("loop", "rep"), None),
        P(("loop", "rep"), None),
    )
    return jax.shard_map(
        local, mesh=mesh, in_specs=placed, out_specs=P(("loop", "rep"), None), check_vma=False
    )
```

time: 457 us -> 99.2 us (0.22)
  the two profiles are of different devices: /device:TPU:7 before, /device:TPU:16 now
where the time goes in v1:
time: 99.2 us; the launch traced here: 98.8 us
  Pallas kernels  95.8 us (97%)
  local copies, waits for them, and re-layouts  2.95 us (3%)
    pallas_call x1, Pallas kernels, gather(): pl.pallas_call(gather_kernel, out_shape=jax.ShapeDtypeStruct((NX * NC, 2,...  55.4 us
    pallas_call x1, Pallas kernels, combine(): pl.pallas_call(combine_kernel, out_shape=jax.ShapeDtypeStruct((rows, weig...  32 us
    pallas_call x1, Pallas kernels, products(): pl.pallas_call(functools.partial(product_kernel, slots=slots, blocks=bloc...  8.44 us
    unnamed x2, local copies, waits for them, and re-layouts  2.25 us

profile of v1, /device:TPU:16, one launch (start us, length us, event | category | flops | bytes accessed | tf_op | source)
XLA Modules:
  0.0 98.8 jit_solution(15470128897305756217)
XLA Ops:
  0.0 0.8 copy.6
  0.8 0.7 reshape.16.coords
  1.5 55.4 %gather.1 = bf16[8,2,4,128,256]{4,3,2,1,0:T(8,128)(2,1)} custom-call(bf16[128,256]{1,0:T(8,128)(2,1)} %own.1), custom_call_target="tpu_custom_call" | custom-call | tf_op jit(solution)/shard_map/gather/pallas_call | solution.py:265
  56.9 8.4 %products.1 = bf16[8,128,256]{2,1,0:T(8,128)(2,1)} custom-call(s32[8]{0:T(128)} %bitcast.6, s32[192]{0:T(256)} %reshape.16.coords, s32[1]{0:T(128)} %bitcast.1.first, bf16[96,128,128]{2,1,0:T(8,128)(2,1)} %tiles.1, bf16[8,8,128,256]{3,2,1,0:T(8,128)(2,1)} %bitcast.4), custom_call_target="tpu_custom_call" | custom-call | tf_op jit(solution)/shard_map/products/pallas_call | solution.py:326
  65.3 32.0 %combine.1 = bf16[128,256]{1,0:T(8,128)(2,1)} custom-call(bf16[4,2,128,256]{3,2,1,0:T(8,128)(2,1)} %bitcast.5, bf16[256,256]{1,0:T(8,128)(2,1)} %weight.1), custom_call_target="tpu_custom_call" | custom-call | tf_op jit(solution)/shard_map/combine/pallas_call | solution.py:377
  97.3 1.5 %copy.8 = bf16[128,256]{1,0:T(8,128)(2,1)} copy(bf16[128,256]{1,0:T(8,128)(2,1)} %combine.1) | data formatting | bytes 131072

commit v2 on v0

v2 whole, which is shorter than its diff:
```python
import functools

import jax
import jax.numpy as jnp
from jax import lax
from jax.experimental import pallas as pl
from jax.experimental.pallas import tpu as pltpu
from jax.sharding import PartitionSpec as P

MESH = pl.DeviceIdType.MESH
NX, NY, NZ, NC, NZH, NZL = 4, 4, 16, 2, 2, 8
STEPS = NX * NC
BLOCKS = NY * NZH
FAR = NZ // 2
PIECES = 2
LANES = 128
WIDE = NY // PIECES
Y_LAG, F_LAG = 2, 6


def place():
    l = lax.axis_index("loop")
    r = lax.axis_index("rep")
    zl, x, core = l // (NX * NC), (l // NC) % NX, l % NC
    y, zh = r // NZH, r % NZH
    return x, core, y, zh * NZL + zl


def device(x, core, y, z):
    return ((z % NZL) * (NX * NC) + x * NC + core, y * NZH + z // NZL)


def remote(src, dst, send, recv, target):
    return pltpu.make_async_remote_copy(
        src_ref=src, dst_ref=dst, send_sem=send, recv_sem=recv,
        device_id=target, device_id_type=MESH,
    )


def layer_kernel(
    counts, coords, own, weight_in, tiles_in, out,
    home, near, across, beyond, up, down, tiles, sums, give, got, hold, z_give, z_got,
    weight, draft, table,
    up_send, up_recv, down_send, down_recv, y_send, y_recv, y_local,
    x_send, x_recv, f_send, f_recv, s_send, s_recv,
    g_send, g_recv, z_send, z_recv, t_sem, w_sem, d_sem, *, slots,
):
    x, core, y, z = place()
    zl, zh = z % NZL, z // NZL
    right = device((x + 1) % NX, core, y, z)
    left = device((x + NX - 1) % NX, core, y, z)
    above = device(x, core, y, (z + 1) % NZ)
    below = device(x, core, y, (z + NZ - 1) % NZ)
    sibling = device(x, 1 - core, y, z)
    partner = device(x, core, y, (z + NZL) % NZ)
    others = [(y + d) % NY for d in range(1, NY)]
    def group(half):
        return pl.ds(half * NY, NY)

    tile_copy = pltpu.make_async_copy(tiles_in, tiles, t_sem)
    tile_copy.start()
    weight_copy = pltpu.make_async_copy(weight_in, weight, w_sem)
    weight_copy.start()

    barrier = pltpu.get_barrier_semaphore()
    friends = [right, left, above, below, sibling]
    friends += [device(x, core, v, z) for v in others]
    friends += [device(x, core, y, (z + d) % NZ) for d in (2, NZ - 2)]
    for friend in friends:
        pl.semaphore_signal(barrier, inc=1, device_id=friend, device_id_type=MESH)
    pl.semaphore_wait(barrier, len(friends))

    def z_copy(src, step, hops, upward):
        if upward:
            return remote(
                src, up.at[step], up_send.at[step], up_recv.at[step],
                device(x, core, y, (z + hops) % NZ),
            )
        return remote(
            src, down.at[step], down_send.at[step], down_recv.at[step],
            device(x, core, y, (z + NZ - hops) % NZ),
        )

    def goes(plane):
        offset = (zl + NZL - zh + NZL - plane % NZL) % NZL
        return offset // 2, offset % 2, plane // NZL

    def y_copy(src, plane, index):
        reader, kind, half = goes(plane)
        return remote(
            src, home.at[kind, half * NY + y], y_send.at[index], y_recv.at[kind * 2 + half, y],
            device(x, core, reader, z),
        )

    def hand_on(src, plane, index):
        reader, kind, half = goes(plane)

        @pl.when(reader == y)
        def _():
            pltpu.make_async_copy(
                src, home.at[kind, half * NY + y], y_local.at[kind * 2 + half]
            ).start()

        @pl.when(reader != y)
        def _():
            y_copy(src, plane, index).start()

    def x_copy(kind, half, direction, piece):
        at = pl.ds(half * NY + piece * WIDE, WIDE)
        return remote(
            home.at[kind, at], near.at[direction, at],
            x_send.at[direction, kind * 2 + half, piece], x_recv.at[direction, half, piece],
            right if direction == 0 else left,
        )

    def forward(direction, half, piece):
        at = pl.ds(half * NY + piece * WIDE, WIDE)
        return remote(
            near.at[direction, at], across.at[0, at],
            f_send.at[direction, half, piece], f_recv.at[half, piece],
            right if direction == 0 else left,
        )

    def share(index, src, dst, half):
        return remote(
            src.at[group(half)], dst.at[group(half)], s_send.at[index, half], s_recv.at[index, half],
            sibling,
        )

    def share_home(kind, half):
        return share(0, home.at[kind], home.at[2], half)

    def share_near(direction, half):
        return share(1 + direction, near.at[direction], near.at[2 + direction], half)

    def share_across(half):
        return share(3, across.at[0], beyond.at[0], half)

    def sends(kind, direction):
        inner = (x < NX - 1) if direction == 0 else (x > 0)
        outer = (x == NX - 1) if direction == 0 else (x == 0)
        chosen = jnp.where(kind == direction, inner.astype(jnp.int32), outer.astype(jnp.int32))
        return chosen == 1

    def complete(plane):
        reader, kind, half = goes(plane)

        @pl.when(reader == y)
        def _():
            for v in others:
                remote(
                    own, home.at[kind, half * NY + v], y_send.at[0],
                    y_recv.at[kind * 2 + half, v], sibling,
                ).wait_recv()
            pltpu.make_async_copy(
                own, home.at[kind, half * NY + y], y_local.at[kind * 2 + half]
            ).wait()
            for direction in range(2):
                @pl.when(sends(kind, direction))
                def _():
                    for piece in range(PIECES):
                        x_copy(kind, half, direction, piece).start()

            @pl.when(kind == core)
            def _():
                share_home(kind, half).start()

    moves = ((0, 0, x < NX - 1), (0, 1, x == 2), (1, 1, x > 0), (1, 0, x == 1))
    kind_from = (jnp.where(x > 0, 0, 1), jnp.where(x < NX - 1, 1, 0))

    def pass_on(plane):
        reader, kind, half = goes(plane)
        for source in range(2):
            @pl.when((reader == y) & (kind == kind_from[source]))
            def _():
                for place_of in range(PIECES):
                    x_copy(kind, half, source, place_of).wait_recv()
                    for direction, piece, when in moves:
                        if direction == source and piece == place_of:
                            @pl.when(when)
                            def _():
                                forward(direction, half, piece).start()
                share_near(source, half).start()

    for hops in (2, 1):
        z_copy(own, hops, hops, True).start()
        z_copy(own, hops, hops, False).start()
    hand_on(own, z, 0)

    def at_lag(t, lag, act):
        @pl.when(t == lag)
        def _():
            act(z)

        @pl.when((t > lag) & (t < lag + FAR))
        def _():
            act((z + NZ - t + lag) % NZ)
            act((z + t - lag) % NZ)

        @pl.when(t == lag + FAR)
        def _():
            act((z + FAR) % NZ)

    def z_step(t):
        z_copy(own, t, 1, True).wait_recv()

        @pl.when((t % 2 == 0) & (t < FAR))
        def _():
            z_copy(up.at[t], t + 2, 2, True).start()
            z_copy(up.at[t], t + 1, 1, True).start()

        @pl.when(t < FAR)
        def _():
            z_copy(own, t, 1, False).wait_recv()

            @pl.when(t % 2 == 0)
            def _():
                @pl.when(t < FAR - 2)
                def _():
                    z_copy(down.at[t], t + 2, 2, False).start()

                z_copy(down.at[t], t + 1, 1, False).start()

        hand_on(up.at[t], (z + NZ - t) % NZ, t)

        @pl.when(t < FAR)
        def _():
            hand_on(down.at[t], (z + t) % NZ, FAR + t)

    def loop_body(t, carry):
        @pl.when(t <= FAR)
        def _():
            z_step(t)

        at_lag(t, Y_LAG, complete)
        at_lag(t, F_LAG, pass_on)
        return carry

    entries = STEPS * slots
    lanes = draft.shape[1]
    lane = lax.broadcasted_iota(jnp.int32, (1, lanes), 1)
    deep = lax.broadcasted_iota(jnp.int32, (lanes, lanes), 0)
    wide = lax.broadcasted_iota(jnp.int32, (lanes, lanes), 1)

    def upright(line):
        spread = jnp.where(deep == wide, jnp.broadcast_to(line, (lanes, lanes)), 0)
        return jnp.sum(spread, axis=1, keepdims=True)

    def falling(grid):
        return jnp.sum(grid, axis=0, keepdims=True)

    of_step = lane // slots
    slot = lane - of_step * slots
    limit = jnp.zeros_like(lane)
    for s in range(STEPS):
        limit = jnp.where(of_step == s, counts[0, s], limit)
    row_block = jnp.where(slot < limit, coords[0:1, :], BLOCKS)
    column_block = coords[1:2, :]
    key = of_step * (2 * BLOCKS) + row_block
    full = key * lanes + lane
    key_up = upright(key)
    rank_up = jnp.sum(
        (jnp.broadcast_to(full, (lanes, lanes)) < upright(full)).astype(jnp.int32),
        axis=1, keepdims=True,
    )
    hit = rank_up == wide
    order = falling(jnp.where(hit, deep, 0))
    spot_up = upright((column_block % NZH) * NY + column_block // NZH)
    ranked = falling(jnp.where(hit, key_up, 0))
    follows = (ranked == pltpu.roll(ranked, 1, 1)) & (lane > 0)
    goal = (lane // BLOCKS) * (2 * BLOCKS) + lane % BLOCKS
    upto = falling(((key_up <= goal) & (deep < entries)).astype(jnp.int32))
    some = falling(((key_up == goal) & (deep < entries)).astype(jnp.int32))
    draft[0:1, :] = order
    draft[1:2, :] = falling(jnp.where(hit, spot_up, 0))
    draft[2:3, :] = follows.astype(jnp.int32)
    draft[3:4, :] = jnp.where(some > 0, upto, 0)
    table_copy = pltpu.make_async_copy(draft, table, d_sem)

    def multiply(ref, index, step):
        for k in range(slots):
            e = step * slots + k
            product = jnp.dot(
                tiles[table[0, e]], ref[index, table[1, e]],
                preferred_element_type=jnp.float32,
            )
            if k > 0:
                product += jnp.where(table[2, e] == 1, sums[e], 0.0)
            sums[e + 1] = product

    def step_of(shared, rel):
        other = (rel * 2 + STEPS - 1 + core * 2) % STEPS
        return jnp.where(shared == 1, other, rel * 2)

    lax.fori_loop(1, FAR + Y_LAG + 1, loop_body, 0)
    sums[0] = jnp.zeros(sums.shape[1:], sums.dtype)
    table_copy.start()
    table_copy.wait()
    tile_copy.wait()
    weight_copy.wait()
    for half in range(2):
        share(0, home.at[0], home.at[2], half).wait_recv()

    def home_body(i, carry):
        multiply(home, i * 2, step_of(i, 0))
        return carry

    lax.fori_loop(0, 2, home_body, 0)
    lax.fori_loop(FAR + Y_LAG + 1, FAR + F_LAG + 1, loop_body, 0)
    for half in range(2):
        for direction in range(2):
            share_near(direction, half).wait_recv()

    def near_body(i, carry):
        multiply(near, i, step_of(i // 2, 1 + 2 * (i % 2)))
        return carry

    lax.fori_loop(0, 4, near_body, 0)
    for half in range(2):
        for piece in range(2):
            forward(0, half, piece).wait_recv()
        share_across(half).start()
    multiply(across, 0, step_of(0, 2))
    for half in range(2):
        share_across(half).wait_recv()
    multiply(beyond, 0, step_of(1, 2))

    def total(block):
        held = sums[table[3, block]]
        for step in range(1, STEPS):
            held += sums[table[3, block + step * BLOCKS]]
        return held

    def g_copy(turn, i):
        return remote(
            give.at[turn, i], got.at[turn, i], g_send.at[turn, i], g_recv.at[turn, i],
            device(x, core, others[i], z),
        )

    halves = (1 - zh, zh)
    for turn in range(2):
        for i in range(NY - 1):
            give[turn, i] = total(others[i] * NZH + halves[turn]).astype(give.dtype)
            g_copy(turn, i).start()
    to_partner = remote(z_give, z_got, z_send, z_recv, partner)
    for turn in range(2):
        hold[...] = total(y * NZH + halves[turn])
        for i in range(NY - 1):
            g_copy(turn, i).wait_recv()
        held = hold[...]
        for i in range(NY - 1):
            held += got[turn, i].astype(jnp.float32)
        if turn == 0:
            z_give[...] = held.astype(z_give.dtype)
            to_partner.start()
        else:
            hold[...] = held
    to_partner.wait()
    aggregated = (hold[...] + z_got[...].astype(jnp.float32)).astype(weight.dtype)
    product = jnp.dot(aggregated, weight[...], preferred_element_type=jnp.float32)
    out[...] = jnp.maximum(product, 0.0).astype(out.dtype)

    for turn in range(2):
        for i in range(NY - 1):
            g_copy(turn, i).wait_send()
    for half in range(2):
        share(0, home.at[0], home.at[2], half).wait_send()
        share_across(half).wait_send()
        for direction in range(2):
            share_near(direction, half).wait_send()
            for kind in range(2):
                @pl.when(sends(kind, direction))
                def _():
                    for piece in range(PIECES):
                        x_copy(kind, half, direction, piece).wait_send()
        for direction, piece, when in moves:
            @pl.when(when)
            def _():
                forward(direction, half, piece).wait_send()

    def hand_on_done(src, plane, index):
        @pl.when(goes(plane)[0] != y)
        def _():
            y_copy(src, plane, index).wait_send()

    hand_on_done(own, z, 0)

    def drain(t, carry):
        hand_on_done(up.at[t], (z + NZ - t) % NZ, t)
        z_copy(own, t, 1, True).wait_send()

        @pl.when(t < FAR)
        def _():
            hand_on_done(down.at[t], (z + t) % NZ, FAR + t)
            z_copy(own, t, 1, False).wait_send()

        return carry

    lax.fori_loop(1, FAR + 1, drain, 0)


def local(features, weight, tile_values, tile_coords, tile_counts):
    rows, width = features.shape
    slots = tile_values.shape[0] // STEPS
    coords = jnp.pad(tile_coords.T, ((0, 0), (0, LANES - tile_coords.shape[0])))
    dma = pltpu.SemaphoreType.DMA
    kind = features.dtype
    vmem = pl.BlockSpec(memory_space=pltpu.VMEM)
    hbm = pl.BlockSpec(memory_space=pl.ANY)
    return pl.pallas_call(
        functools.partial(layer_kernel, slots=slots),
        out_shape=jax.ShapeDtypeStruct((rows, weight.shape[1]), kind),
        in_specs=[
            pl.BlockSpec(memory_space=pltpu.SMEM), vmem, hbm, hbm, hbm,
        ],
        out_specs=vmem,
        scratch_shapes=[
            pltpu.VMEM((3, BLOCKS, rows, width), kind),
            pltpu.VMEM((4, BLOCKS, rows, width), kind),
            pltpu.VMEM((1, BLOCKS, rows, width), kind),
            pltpu.VMEM((1, BLOCKS, rows, width), kind),
            pltpu.VMEM((FAR + 1, rows, width), kind),
            pltpu.VMEM((FAR, rows, width), kind),
            pltpu.VMEM(tile_values.shape, kind),
            pltpu.VMEM((STEPS * slots + 1, rows, width), jnp.float32),
            pltpu.VMEM((2, NY - 1, rows, width), kind),
            pltpu.VMEM((2, NY - 1, rows, width), kind),
            pltpu.VMEM((rows, width), jnp.float32),
            pltpu.VMEM((rows, width), kind),
            pltpu.VMEM((rows, width), kind),
            pltpu.VMEM(weight.shape, kind),
            pltpu.VMEM((8, LANES), jnp.int32),
            pltpu.SMEM((8, LANES), jnp.int32),
            dma((FAR + 1,)), dma((FAR + 1,)), dma((FAR,)), dma((FAR,)),
            dma((NZ,)), dma((4, NY)), dma((4,)),
            dma((2, 4, PIECES)), dma((2, 2, PIECES)), dma((2, 2, PIECES)), dma((2, PIECES)),
            dma((4, 2)), dma((4, 2)),
            dma((2, NY - 1)), dma((2, NY - 1)), dma, dma, dma, dma, dma,
        ],
        compiler_params=pltpu.CompilerParams(
            collective_id=0, has_side_effects=True, vmem_limit_bytes=60 * 1024 * 1024
        ),
        name="layer",
    )(tile_counts, coords, features, weight, tile_values)


def solution(mesh):
    placed = (
        P(("loop", "rep"), None),
        P(),
        P(("loop", "rep"), None, None),
        P(("loop", "rep"), None),
        P(("loop", "rep"), None),
    )
    return jax.shard_map(
        local, mesh=mesh, in_specs=placed, out_specs=P(("loop", "rep"), None), check_vma=False
    )
```

time: 457 us -> 81.2 us (0.18)
  waiting for transfers between devices: 234 us -> 0 us
  blocking collectives: 83 us -> 0 us
  Pallas kernels: 0 us -> 76.9 us
  starting transfers between devices: 45.9 us -> 0 us
  other arithmetic: 34.3 us -> 0 us
  local copies, waits for them, and re-layouts: 26.7 us -> 2.72 us
  matrix products: 15.9 us -> 0 us
  between operations: 13.9 us -> 0.01 us
    reduce_scatter x1 -> x0, waiting for transfers between devices: 149 us -> none  [local(): lax.psum_scatter(running.reshape(block_count * tile_size, feat_width), 'r...]
    ppermute x10 -> x0, waiting for transfers between devices: 85.3 us -> none  [from_behind(): return lax.ppermute(x, axis, [(i, (i + by) % count) for i in range(count)])]
    all_gather x1 -> x0, blocking collectives: 83 us -> none  [local(): current_slab = lax.all_gather(features, 'rep', axis=0, tiled=True)]
    pallas_call x0 -> x1, Pallas kernels: none -> 76.9 us  [local(): pl.pallas_call(functools.partial(layer_kernel, slots=slots), out_shape=ja...]
    ppermute x10 -> x0, starting transfers between devices: 45.9 us -> none  [from_behind(): return lax.ppermute(x, axis, [(i, (i + by) % count) for i in range(count)])]
    scatter-add x8 -> x0, other arithmetic: 22.4 us -> none  [local(): running.at[coords[step_index, :, 0]]]
    dot_general x9 -> x0, matrix products: 15.9 us -> none  [the longest x8 14.2 us: local(): jnp.einsum('ktc,kcf->ktf', values[step_index], pieces, preferred_element_...]
    mul x8 -> x0, local copies, waits for them, and re-layouts: 13.5 us -> none  [local(): products * live_slot[:, None, None]]
  transfers between devices with their start and end apart: 11 -> 0, of which waited for: 7 -> 0; matrix products, arithmetic and copies ran while one was open for 15% -> 0% of each run, Pallas kernels for 0% -> 0%
where the time goes in v2:
time: 81.2 us; the launch traced here: 79.7 us
  Pallas kernels  76.9 us (95%)
  local copies, waits for them, and re-layouts  2.72 us (3%)
    pallas_call x1, Pallas kernels, local(): pl.pallas_call(functools.partial(layer_kernel, slots=slots), out_shape=ja...  76.9 us

profile of v2, /device:TPU:7, one launch (start us, length us, event | category | flops | bytes accessed | tf_op | source)
XLA Modules:
  0.0 79.7 jit_solution(14014765281176857151)
XLA Ops:
  0.0 1.2 %pad.4.coords = s32[2,128]{1,0:T(2,128)} pad(s32[2,96]{1,0:T(2,128)} %bitcast.1, s32[]{:T(128)} %constant.0.clone.1), padding=0_0x0_32 | pad | bytes 1796 | tf_op jit(solution)/shard_map/jit(_pad)/pad | solution.py:405
  1.2 76.9 %layer.1 = bf16[128,256]{1,0:T(8,128)(2,1)} custom-call(s32[1,8]{1,0:T(1,128)} %counts.1, s32[2,128]{1,0:T(2,128)} %pad.4.coords, bf16[128,256]{1,0:T(8,128)(2,1)} %own.1, bf16[256,256]{1,0:T(8,128)(2,1)} %weight_in.1, bf16[96,128,128]{2,1,0:T(8,128)(2,1)} %tiles_in.1), custom_call_target="tpu_custom_call" | custom-call | tf_op jit(solution)/shard_map/layer/pallas_call | solution.py:410
  78.2 1.5 %copy.7 = bf16[128,256]{1,0:T(8,128)(2,1)} copy(bf16[128,256]{1,0:T(8,128)(2,1)} %layer.1) | data formatting | bytes 131072

commit v3 on v2

--- a/solution.py
+++ b/solution.py
@@ -13,9 +13,10 @@
 BLOCKS = NY * NZH
 FAR = NZ // 2
 PIECES = 2
+PARTS = 2
 LANES = 128
 WIDE = NY // PIECES
-Y_LAG, F_LAG = 2, 6
+Y_LAG, F_LAG, SYNC = 2, 6, 4
 
 
 def place():
@@ -38,12 +39,12 @@
 
 
 def layer_kernel(
-    counts, coords, own, weight_in, tiles_in, out,
+    counts_in, coords_in, own, weight_in, tiles_in, out,
     home, near, across, beyond, up, down, tiles, sums, give, got, hold, z_give, z_got,
-    weight, draft, table,
+    weight, draft, table, counts, coords, base,
     up_send, up_recv, down_send, down_recv, y_send, y_recv, y_local,
     x_send, x_recv, f_send, f_recv, s_send, s_recv,
-    g_send, g_recv, z_send, z_recv, t_sem, w_sem, d_sem, *, slots,
+    g_send, g_recv, z_send, z_recv, t_sem, w_sem, d_sem, c_sem, *, slots,
 ):
     x, core, y, z = place()
     zl, zh = z % NZL, z // NZL
@@ -57,18 +58,21 @@
     def group(half):
         return pl.ds(half * NY, NY)
 
+    small_copies = (
+        pltpu.make_async_copy(counts_in, counts, c_sem.at[0]),
+        pltpu.make_async_copy(coords_in, coords, c_sem.at[1]),
+    )
     tile_copy = pltpu.make_async_copy(tiles_in, tiles, t_sem)
-    tile_copy.start()
     weight_copy = pltpu.make_async_copy(weight_in, weight, w_sem)
-    weight_copy.start()
 
     barrier = pltpu.get_barrier_semaphore()
-    friends = [right, left, above, below, sibling]
+    friends = [right, left, above, below]
     friends += [device(x, core, v, z) for v in others]
     friends += [device(x, core, y, (z + d) % NZ) for d in (2, NZ - 2)]
     for friend in friends:
         pl.semaphore_signal(barrier, inc=1, device_id=friend, device_id_type=MESH)
-    pl.semaphore_wait(barrier, len(friends))
+    pl.semaphore_wait(barrier, len(friends) + core)
+    pl.semaphore_signal(barrier, inc=1, device_id=sibling, device_id_type=MESH)
 
     def z_copy(src, step, hops, upward):
         if upward:
@@ -161,9 +165,12 @@
                     for piece in range(PIECES):
                         x_copy(kind, half, direction, piece).start()
 
-            @pl.when(kind == core)
-            def _():
-                share_home(kind, half).start()
+    def share_own(plane):
+        reader, kind, half = goes(plane)
+
+        @pl.when((reader == y) & (kind == core))
+        def _():
+            share_home(kind, half).start()
 
     moves = ((0, 0, x < NX - 1), (0, 1, x == 2), (1, 1, x > 0), (1, 0, x == 1))
     kind_from = (jnp.where(x > 0, 0, 1), jnp.where(x < NX - 1, 1, 0))
@@ -186,6 +193,10 @@
         z_copy(own, hops, hops, True).start()
         z_copy(own, hops, hops, False).start()
     hand_on(own, z, 0)
+    for copy in small_copies:
+        copy.start()
+    tile_copy.start()
+    weight_copy.start()
 
     def at_lag(t, lag, act):
         @pl.when(t == lag)
@@ -233,9 +244,30 @@
             z_step(t)
 
         at_lag(t, Y_LAG, complete)
+
+        @pl.when(t == SYNC)
+        def _():
+            @pl.when(core == 0)
+            def _():
+                pl.semaphore_wait(barrier, 1)
+
+            share_own(z)
+
+            def earlier(d, nothing):
+                share_own((z + d) % NZ)
+                share_own((z + NZ - d) % NZ)
+                return nothing
+
+            lax.fori_loop(1, SYNC - Y_LAG + 1, earlier, 0)
+
+        @pl.when(t > SYNC)
+        def _():
+            at_lag(t, Y_LAG, share_own)
+
         at_lag(t, F_LAG, pass_on)
         return carry
 
+    rows = own.shape[0]
     entries = STEPS * slots
     lanes = draft.shape[1]
     lane = lax.broadcasted_iota(jnp.int32, (1, lanes), 1)
@@ -249,13 +281,17 @@
     def falling(grid):
         return jnp.sum(grid, axis=0, keepdims=True)
 
+    for copy in small_copies:
+        copy.wait()
+    pad = jnp.zeros((2, lanes - entries), jnp.int32)
+    places = jnp.concatenate([coords[...], pad], axis=1)
     of_step = lane // slots
     slot = lane - of_step * slots
     limit = jnp.zeros_like(lane)
     for s in range(STEPS):
         limit = jnp.where(of_step == s, counts[0, s], limit)
-    row_block = jnp.where(slot < limit, coords[0:1, :], BLOCKS)
-    column_block = coords[1:2, :]
+    row_block = jnp.where(slot < limit, places[0:1, :], BLOCKS)
+    column_block = places[1:2, :]
     key = of_step * (2 * BLOCKS) + row_block
     full = key * lanes + lane
     key_up = upright(key)
@@ -290,7 +326,7 @@
 
     def step_of(shared, rel):
         other = (rel * 2 + STEPS - 1 + core * 2) % STEPS
-        return jnp.where(shared == 1, other, rel * 2)
+        return shared * other + (1 - shared) * rel * 2
 
     lax.fori_loop(1, FAR + Y_LAG + 1, loop_body, 0)
     sums[0] = jnp.zeros(sums.shape[1:], sums.dtype)
@@ -316,6 +352,17 @@
         return carry
 
     lax.fori_loop(0, 4, near_body, 0)
+    early = [step_of(shared, rel) for shared in range(2) for rel in (0, 1, 3)]
+    late = [step_of(shared, 2) for shared in range(2)]
+
+    def base_body(block, carry):
+        held = sums[table[3, block + early[0] * BLOCKS]]
+        for step in early[1:]:
+            held += sums[table[3, block + step * BLOCKS]]
+        base[block] = held
+        return carry
+
+    lax.fori_loop(0, BLOCKS, base_body, 0)
     for half in range(2):
         for piece in range(2):
             forward(0, half, piece).wait_recv()
@@ -325,44 +372,58 @@
         share_across(half).wait_recv()
     multiply(beyond, 0, step_of(1, 2))
 
-    def total(block):
-        held = sums[table[3, block]]
-        for step in range(1, STEPS):
-            held += sums[table[3, block + step * BLOCKS]]
+    span = rows // PARTS
+
+    def total(block, at):
+        held = base[block, at]
+        for step in late:
+            held += sums[table[3, block + step * BLOCKS], at]
         return held
 
-    def g_copy(turn, i):
+    def g_copy(turn, i, p):
+        at = pl.ds(p * span, span)
         return remote(
-            give.at[turn, i], got.at[turn, i], g_send.at[turn, i], g_recv.at[turn, i],
-            device(x, core, others[i], z),
+            give.at[turn, i, at], got.at[turn, i, at], g_send.at[turn, i, p],
+            g_recv.at[turn, i, p], device(x, core, others[i], z),
         )
 
+    def across_z(p):
+        at = pl.ds(p * span, span)
+        return remote(z_give.at[at], z_got.at[at], z_send.at[p], z_recv.at[p], partner)
+
     halves = (1 - zh, zh)
+    cuts = [pl.ds(p * span, span) for p in range(PARTS)]
+    for turn in range(2):
+        for p in range(PARTS):
+            for i in range(NY - 1):
+                give[turn, i, cuts[p]] = total(
+                    others[i] * NZH + halves[turn], cuts[p]
+                ).astype(give.dtype)
+                g_copy(turn, i, p).start()
+
+    def gathered(turn, p):
+        held = total(y * NZH + halves[turn], cuts[p])
+        for i in range(NY - 1):
+            g_copy(turn, i, p).wait_recv()
+        for i in range(NY - 1):
+            held += got[turn, i, cuts[p]].astype(jnp.float32)
+        return held
+
+    for p in range(PARTS):
+        z_give[cuts[p]] = gathered(0, p).astype(z_give.dtype)
+        across_z(p).start()
+    for p in range(PARTS):
+        hold[cuts[p]] = gathered(1, p)
+    for p in range(PARTS):
+        across_z(p).wait()
+        aggregated = (hold[cuts[p]] + z_got[cuts[p]].astype(jnp.float32)).astype(weight.dtype)
+        product = jnp.dot(aggregated, weight[...], preferred_element_type=jnp.float32)
+        out[cuts[p]] = jnp.maximum(product, 0.0).astype(out.dtype)
+
     for turn in range(2):
         for i in range(NY - 1):
-            give[turn, i] = total(others[i] * NZH + halves[turn]).astype(give.dtype)
-            g_copy(turn, i).start()
-    to_partner = remote(z_give, z_got, z_send, z_recv, partner)
-    for turn in range(2):
-        hold[...] = total(y * NZH + halves[turn])
-        for i in range(NY - 1):
-            g_copy(turn, i).wait_recv()
-        held = hold[...]
-        for i in range(NY - 1):
-            held += got[turn, i].astype(jnp.float32)
-        if turn == 0:
-            z_give[...] = held.astype(z_give.dtype)
-            to_partner.start()
-        else:
-            hold[...] = held
-    to_partner.wait()
-    aggregated = (hold[...] + z_got[...].astype(jnp.float32)).astype(weight.dtype)
-    product = jnp.dot(aggregated, weight[...], preferred_element_type=jnp.float32)
-    out[...] = jnp.maximum(product, 0.0).astype(out.dtype)
-
-    for turn in range(2):
-        for i in range(NY - 1):
-            g_copy(turn, i).wait_send()
+            for p in range(PARTS):
+                g_copy(turn, i, p).wait_send()
     for half in range(2):
         share(0, home.at[0], home.at[2], half).wait_send()
         share_across(half).wait_send()
@@ -402,16 +463,15 @@
 def local(features, weight, tile_values, tile_coords, tile_counts):
     rows, width = features.shape
     slots = tile_values.shape[0] // STEPS
-    coords = jnp.pad(tile_coords.T, ((0, 0), (0, LANES - tile_coords.shape[0])))
     dma = pltpu.SemaphoreType.DMA
     kind = features.dtype
     vmem = pl.BlockSpec(memory_space=pltpu.VMEM)
-    hbm = pl.BlockSpec(memory_space=pl.ANY)
+    hbm = pl.BlockSpec(memory_space=pltpu.HBM)
     return pl.pallas_call(
         functools.partial(layer_kernel, slots=slots),
         out_shape=jax.ShapeDtypeStruct((rows, weight.shape[1]), kind),
         in_specs=[
-            pl.BlockSpec(memory_space=pltpu.SMEM), vmem, hbm, hbm, hbm,
+            hbm, hbm, hbm, hbm, hbm,
         ],
         out_specs=vmem,
         scratch_shapes=[
@@ -431,17 +491,21 @@
             pltpu.VMEM(weight.shape, kind),
             pltpu.VMEM((8, LANES), jnp.int32),
             pltpu.SMEM((8, LANES), jnp.int32),
+            pltpu.SMEM(tile_counts.shape, jnp.int32),
+            pltpu.VMEM(tile_coords.T.shape, jnp.int32),
+            pltpu.VMEM((BLOCKS, rows, width), jnp.float32),
             dma((FAR + 1,)), dma((FAR + 1,)), dma((FAR,)), dma((FAR,)),
             dma((NZ,)), dma((4, NY)), dma((4,)),
             dma((2, 4, PIECES)), dma((2, 2, PIECES)), dma((2, 2, PIECES)), dma((2, PIECES)),
             dma((4, 2)), dma((4, 2)),
-            dma((2, NY - 1)), dma((2, NY - 1)), dma, dma, dma, dma, dma,
+            dma((2, NY - 1, PARTS)), dma((2, NY - 1, PARTS)), dma((PARTS,)), dma((PARTS,)),
+            dma, dma, dma, dma((2,)),
         ],
         compiler_params=pltpu.CompilerParams(
             collective_id=0, has_side_effects=True, vmem_limit_bytes=60 * 1024 * 1024
         ),
         name="layer",
-    )(tile_counts, coords, features, weight, tile_values)
+    )(tile_counts, tile_coords.T, features, weight, tile_values)
 
 
 def solution(mesh):

time: 81.2 us -> 78.7 us (0.969); the launches traced: 79.7 us -> 78.5 us
  local copies, waits for them, and re-layouts: 2.72 us -> 1.47 us
    pad x1 -> x0, local copies, waits for them, and re-layouts: 1.24 us -> none  [local(): coords = jnp.pad(tile_coords.T, ((0, 0), (0, LANES - tile_coords.shape[0])))]
where the time goes in v3:
time: 78.7 us; the launch traced here: 78.5 us
  Pallas kernels  77 us (98%)
  local copies, waits for them, and re-layouts  1.47 us (2%)
    pallas_call x1, Pallas kernels, local(): pl.pallas_call(functools.partial(layer_kernel, slots=slots), out_shape=ja...  77 us

profile of v3, /device:TPU:7, one launch (start us, length us, event | category | flops | bytes accessed | tf_op | source)
XLA Modules:
  0.0 78.5 jit_solution(6320425298353695066)
XLA Ops:
  0.0 77.0 %layer.1 = bf16[128,256]{1,0:T(8,128)(2,1)} custom-call(s32[1,8]{1,0:T(1,128)} %counts_in.1, s32[2,96]{1,0:T(2,128)} %bitcast.1, bf16[128,256]{1,0:T(8,128)(2,1)} %own.1, bf16[256,256]{1,0:T(8,128)(2,1)} %weight_in.1, bf16[96,128,128]{2,1,0:T(8,128)(2,1)} %tiles_in.1), custom_call_target="tpu_custom_call" | custom-call | tf_op jit(solution)/shard_map/layer/pallas_call | solution.py:470
  77.0 1.5 %copy.7 = bf16[128,256]{1,0:T(8,128)(2,1)} copy(bf16[128,256]{1,0:T(8,128)(2,1)} %layer.1) | data formatting | bytes 131072

commit v4 on v3

--- a/solution.py
+++ b/solution.py
@@ -13,6 +13,7 @@
 BLOCKS = NY * NZH
 FAR = NZ // 2
 PIECES = 2
+CHUNKS = 1
 PARTS = 2
 LANES = 128
 WIDE = NY // PIECES
@@ -74,14 +75,17 @@
     pl.semaphore_wait(barrier, len(friends) + core)
     pl.semaphore_signal(barrier, inc=1, device_id=sibling, device_id_type=MESH)
 
-    def z_copy(src, step, hops, upward):
+    grain = own.shape[0] // CHUNKS
+
+    def z_copy(src, step, hops, upward, chunk):
+        at = pl.ds(chunk * grain, grain)
         if upward:
             return remote(
-                src, up.at[step], up_send.at[step], up_recv.at[step],
+                src.at[at], up.at[step, at], up_send.at[step, chunk], up_recv.at[step, chunk],
                 device(x, core, y, (z + hops) % NZ),
             )
         return remote(
-            src, down.at[step], down_send.at[step], down_recv.at[step],
+            src.at[at], down.at[step, at], down_send.at[step, chunk], down_recv.at[step, chunk],
             device(x, core, y, (z + NZ - hops) % NZ),
         )
 
@@ -190,53 +194,63 @@
                 share_near(source, half).start()
 
     for hops in (2, 1):
-        z_copy(own, hops, hops, True).start()
-        z_copy(own, hops, hops, False).start()
+        for chunk in range(CHUNKS):
+            z_copy(own, hops, hops, True, chunk).start()
+            z_copy(own, hops, hops, False, chunk).start()
     hand_on(own, z, 0)
     for copy in small_copies:
         copy.start()
     tile_copy.start()
     weight_copy.start()
 
+    def distance(q):
+        return q + 2 * (q % 2) - 1
+
     def at_lag(t, lag, act):
-        @pl.when(t == lag)
+        q = t - lag
+        d = distance(jnp.maximum(q, 1))
+
+        @pl.when(q == 0)
         def _():
             act(z)
 
-        @pl.when((t > lag) & (t < lag + FAR))
-        def _():
-            act((z + NZ - t + lag) % NZ)
-            act((z + t - lag) % NZ)
-
-        @pl.when(t == lag + FAR)
-        def _():
-            act((z + FAR) % NZ)
+        @pl.when((q > 0) & (q <= FAR))
+        def _():
+            act((z + NZ - d) % NZ)
+
+            @pl.when(d < FAR)
+            def _():
+                act((z + d) % NZ)
 
     def z_step(t):
-        z_copy(own, t, 1, True).wait_recv()
-
-        @pl.when((t % 2 == 0) & (t < FAR))
-        def _():
-            z_copy(up.at[t], t + 2, 2, True).start()
-            z_copy(up.at[t], t + 1, 1, True).start()
-
-        @pl.when(t < FAR)
-        def _():
-            z_copy(own, t, 1, False).wait_recv()
-
-            @pl.when(t % 2 == 0)
+        d = distance(t)
+        even = d % 2 == 0
+        for chunk in range(CHUNKS):
+            z_copy(own, d, 1, True, chunk).wait_recv()
+
+            @pl.when(even & (d < FAR))
             def _():
-                @pl.when(t < FAR - 2)
+                z_copy(up.at[d], d + 2, 2, True, chunk).start()
+
+            @pl.when(d < FAR)
+            def _():
+                z_copy(own, d, 1, False, chunk).wait_recv()
+
+                @pl.when(even & (d < FAR - 2))
                 def _():
-                    z_copy(down.at[t], t + 2, 2, False).start()
-
-                z_copy(down.at[t], t + 1, 1, False).start()
-
-        hand_on(up.at[t], (z + NZ - t) % NZ, t)
-
-        @pl.when(t < FAR)
-        def _():
-            hand_on(down.at[t], (z + t) % NZ, FAR + t)
+                    z_copy(down.at[d], d + 2, 2, False, chunk).start()
+
+        @pl.when(even & (d < FAR))
+        def _():
+            for chunk in range(CHUNKS):
+                z_copy(up.at[d], d + 1, 1, True, chunk).start()
+                z_copy(down.at[d], d + 1, 1, False, chunk).start()
+
+        hand_on(up.at[d], (z + NZ - d) % NZ, d)
+
+        @pl.when(d < FAR)
+        def _():
+            hand_on(down.at[d], (z + d) % NZ, FAR + d)
 
     def loop_body(t, carry):
         @pl.when(t <= FAR)
@@ -448,12 +462,14 @@
 
     def drain(t, carry):
         hand_on_done(up.at[t], (z + NZ - t) % NZ, t)
-        z_copy(own, t, 1, True).wait_send()
+        for chunk in range(CHUNKS):
+            z_copy(own, t, 1, True, chunk).wait_send()
 
         @pl.when(t < FAR)
         def _():
             hand_on_done(down.at[t], (z + t) % NZ, FAR + t)
-            z_copy(own, t, 1, False).wait_send()
+            for chunk in range(CHUNKS):
+                z_copy(own, t, 1, False, chunk).wait_send()
 
         return carry
 
@@ -494,7 +510,7 @@
             pltpu.SMEM(tile_counts.shape, jnp.int32),
             pltpu.VMEM(tile_coords.T.shape, jnp.int32),
             pltpu.VMEM((BLOCKS, rows, width), jnp.float32),
-            dma((FAR + 1,)), dma((FAR + 1,)), dma((FAR,)), dma((FAR,)),
+            dma((FAR + 1, CHUNKS)), dma((FAR + 1, CHUNKS)), dma((FAR, CHUNKS)), dma((FAR, CHUNKS)),
             dma((NZ,)), dma((4, NY)), dma((4,)),
             dma((2, 4, PIECES)), dma((2, 2, PIECES)), dma((2, 2, PIECES)), dma((2, PIECES)),
             dma((4, 2)), dma((4, 2)),

time: 78.7 us -> 74.6 us (0.948)
  Pallas kernels: 77 us -> 72.9 us
    pallas_call x1, Pallas kernels: 77 us -> 72.9 us  [local(): pl.pallas_call(functools.partial(layer_kernel, slots=slots), out_shape=ja...]
where the time goes in v4:
time: 74.6 us; the launch traced here: 74.4 us
  Pallas kernels  72.9 us (98%)
  local copies, waits for them, and re-layouts  1.47 us (2%)
    pallas_call x1, Pallas kernels, local(): pl.pallas_call(functools.partial(layer_kernel, slots=slots), out_shape=ja...  72.9 us

profile of v4, /device:TPU:7, one launch (start us, length us, event | category | flops | bytes accessed | tf_op | source)
XLA Modules:
  0.0 74.4 jit_solution(2474545711656314073)
XLA Ops:
  0.0 72.9 %layer.1 = bf16[128,256]{1,0:T(8,128)(2,1)} custom-call(s32[1,8]{1,0:T(1,128)} %counts_in.1, s32[2,96]{1,0:T(2,128)} %bitcast.1, bf16[128,256]{1,0:T(8,128)(2,1)} %own.1, bf16[256,256]{1,0:T(8,128)(2,1)} %weight_in.1, bf16[96,128,128]{2,1,0:T(8,128)(2,1)} %tiles_in.1), custom_call_target="tpu_custom_call" | custom-call | tf_op jit(solution)/shard_map/layer/pallas_call | solution.py:486
  72.9 1.5 %copy.7 = bf16[128,256]{1,0:T(8,128)(2,1)} copy(bf16[128,256]{1,0:T(8,128)(2,1)} %layer.1) | data formatting | bytes 131072

commit v5 on v4

--- a/solution.py
+++ b/solution.py
@@ -141,8 +141,12 @@
     def share_near(direction, half):
         return share(1 + direction, near.at[direction], near.at[2 + direction], half)
 
-    def share_across(half):
-        return share(3, across.at[0], beyond.at[0], half)
+    def share_across(half, piece):
+        at = pl.ds(half * NY + piece * WIDE, WIDE)
+        return remote(
+            across.at[0, at], beyond.at[0, at], s_send.at[3 + piece, half],
+            s_recv.at[3 + piece, half], sibling,
+        )
 
     def sends(kind, direction):
         inner = (x < NX - 1) if direction == 0 else (x > 0)
@@ -280,6 +284,8 @@
 
         at_lag(t, F_LAG, pass_on)
         return carry
+
+    lax.fori_loop(1, 3, loop_body, 0)
 
     rows = own.shape[0]
     entries = STEPS * slots
@@ -342,7 +348,7 @@
         other = (rel * 2 + STEPS - 1 + core * 2) % STEPS
         return shared * other + (1 - shared) * rel * 2
 
-    lax.fori_loop(1, FAR + Y_LAG + 1, loop_body, 0)
+    lax.fori_loop(3, FAR + Y_LAG + 3, loop_body, 0)
     sums[0] = jnp.zeros(sums.shape[1:], sums.dtype)
     table_copy.start()
     table_copy.wait()
@@ -356,7 +362,7 @@
         return carry
 
     lax.fori_loop(0, 2, home_body, 0)
-    lax.fori_loop(FAR + Y_LAG + 1, FAR + F_LAG + 1, loop_body, 0)
+    lax.fori_loop(FAR + Y_LAG + 3, FAR + F_LAG + 1, loop_body, 0)
     for half in range(2):
         for direction in range(2):
             share_near(direction, half).wait_recv()
@@ -380,10 +386,11 @@
     for half in range(2):
         for piece in range(2):
             forward(0, half, piece).wait_recv()
-        share_across(half).start()
+            share_across(half, piece).start()
     multiply(across, 0, step_of(0, 2))
     for half in range(2):
-        share_across(half).wait_recv()
+        for piece in range(PIECES):
+            share_across(half, piece).wait_recv()
     multiply(beyond, 0, step_of(1, 2))
 
     span = rows // PARTS
@@ -409,7 +416,7 @@
     cuts = [pl.ds(p * span, span) for p in range(PARTS)]
     for turn in range(2):
         for p in range(PARTS):
-            for i in range(NY - 1):
+            for i in (1, 0, 2):
                 give[turn, i, cuts[p]] = total(
                     others[i] * NZH + halves[turn], cuts[p]
                 ).astype(give.dtype)
@@ -440,7 +447,8 @@
                 g_copy(turn, i, p).wait_send()
     for half in range(2):
         share(0, home.at[0], home.at[2], half).wait_send()
-        share_across(half).wait_send()
+        for piece in range(PIECES):
+            share_across(half, piece).wait_send()
         for direction in range(2):
             share_near(direction, half).wait_send()
             for kind in range(2):
@@ -513,7 +521,7 @@
             dma((FAR + 1, CHUNKS)), dma((FAR + 1, CHUNKS)), dma((FAR, CHUNKS)), dma((FAR, CHUNKS)),
             dma((NZ,)), dma((4, NY)), dma((4,)),
             dma((2, 4, PIECES)), dma((2, 2, PIECES)), dma((2, 2, PIECES)), dma((2, PIECES)),
-            dma((4, 2)), dma((4, 2)),
+            dma((3 + PIECES, 2)), dma((3 + PIECES, 2)),
             dma((2, NY - 1, PARTS)), dma((2, NY - 1, PARTS)), dma((PARTS,)), dma((PARTS,)),
             dma, dma, dma, dma((2,)),
         ],

time: 74.6 us -> 74.5 us (level)
  no operation moved by 1% of the time
where the time goes in v5:
time: 74.5 us; the launch traced here: 74.3 us
  Pallas kernels  72.8 us (98%)
  local copies, waits for them, and re-layouts  1.47 us (2%)
    pallas_call x1, Pallas kernels, local(): pl.pallas_call(functools.partial(layer_kernel, slots=slots), out_shape=ja...  72.8 us

profile of v5, /device:TPU:7, one launch (start us, length us, event | category | flops | bytes accessed | tf_op | source)
XLA Modules:
  0.0 74.3 jit_solution(8051866404224118503)
XLA Ops:
  0.0 72.8 %layer.1 = bf16[128,256]{1,0:T(8,128)(2,1)} custom-call(s32[1,8]{1,0:T(1,128)} %counts_in.1, s32[2,96]{1,0:T(2,128)} %bitcast.1, bf16[128,256]{1,0:T(8,128)(2,1)} %own.1, bf16[256,256]{1,0:T(8,128)(2,1)} %weight_in.1, bf16[96,128,128]{2,1,0:T(8,128)(2,1)} %tiles_in.1), custom_call_target="tpu_custom_call" | custom-call | tf_op jit(solution)/shard_map/layer/pallas_call | solution.py:494
  72.8 1.5 %copy.7 = bf16[128,256]{1,0:T(8,128)(2,1)} copy(bf16[128,256]{1,0:T(8,128)(2,1)} %layer.1) | data formatting | bytes 131072
